TPU v7x, 32 devices: a whole 2x2x4 slice. The times are simulated.
32 devices in a mesh: groups: 2 (over x), tensor: 16 (over z, y, core).
Axes of the slice: x: 2, y: 2, z: 4, core: 2. Of those that a mesh axis runs over, the one named last changes fastest.
Arguments:
- tokens: bfloat16 [64, 8192], P(('groups', 'tensor')), parts along dimension 0, may hold values from -6 to 6
- cotangent: bfloat16 [64, 8192], P(('groups', 'tensor')), parts along dimension 0, may hold values from -6 to 6
- up_blocks: bfloat16 [512, 128, 128], P('tensor'), may hold values from -0.1875 to 0.1875
- gate_blocks: bfloat16 [512, 128, 128], P('tensor'), may hold values from -0.1875 to 0.1875
- down_blocks: bfloat16 [512, 128, 128], P('tensor'), may hold values from -0.21875 to 0.21875
- up_layout: int32 [512], P('tensor'), may hold values from 0 to 191, as said below
- gate_layout: int32 [512], P('tensor'), may hold values from 0 to 191, as said below
- down_layout: int32 [512], P('tensor'), may hold values from 0 to 191, as said below
- live_counts: int32 [3, 16], P(None, 'tensor'), may hold values from 4 to 32, as said below
Outputs:
- output: bfloat16 [64, 8192], P(('groups', 'tensor')), parts along dimension 0
- grad_tokens: bfloat16 [64, 8192], P(('groups', 'tensor')), parts along dimension 0
- grad_up: bfloat16 [1024, 128, 128], P(('groups', 'tensor')), parts along dimension 0
- grad_gate: bfloat16 [1024, 128, 128], P(('groups', 'tensor')), parts along dimension 0
- grad_down: bfloat16 [1024, 128, 128], P(('groups', 'tensor')), parts along dimension 0
There are 2 independent parts, one for each index of `groups`. A program takes and returns all parts, laid end to end along the dimension named above; an argument that names none is the same for every part. Nothing has to cross between parts.
Inputs may be any that keep to these rules, and one draw needn't show every extreme that they name: `up_layout`: within the 32 slots of one owner the codes of one matrix are all different. `gate_layout`: within the 32 slots of one owner the codes of one matrix are all different. `down_layout`: within the 32 slots of one owner the codes of one matrix are all different. `live_counts`: in each of the three rows some owner has exactly 32 live slots; slots past an owner's count hold blocks that are not used.
All inputs are finite; a program needn't handle non-finite values.
Results may differ from a plain program's by a relative error of at most 0.0051.
Values may be sent and summed in bfloat16 or wider, within the bound.
A program may use at most 64 MiB of HBM per device.

v0:
```python
import jax
import jax.numpy as jnp
from jax import lax
from jax.sharding import PartitionSpec as P

HB_DEV = 3


def slot_tables(layout, count, major_size):
    slot_total = layout.shape[0]
    major = layout // HB_DEV
    minor = layout % HB_DEV
    live_mask = (jnp.arange(slot_total) < count).astype(jnp.float32)
    major_hot = (major[:, None] == jnp.arange(major_size)[None, :]).astype(jnp.float32)
    minor_hot = (minor[:, None] == jnp.arange(HB_DEV)[None, :]).astype(jnp.float32)
    return (major, minor, live_mask, major_hot, minor_hot)


def local(
    tokens,
    cotangent,
    up_blocks,
    gate_blocks,
    down_blocks,
    up_layout,
    gate_layout,
    down_layout,
    live_counts,
):
    highest = lax.Precision.HIGHEST
    f32 = jnp.float32
    x_full = lax.all_gather(tokens, "tensor", axis=0, tiled=True)
    dy_full = lax.all_gather(cotangent, "tensor", axis=0, tiled=True)
    row_total = x_full.shape[0]
    block_size = up_blocks.shape[1]
    width_blocks = x_full.shape[1] // block_size
    x_split = x_full.reshape(row_total, width_blocks, block_size)
    count_trio = live_counts[:, 0]
    up_major, up_minor, up_live, up_rowhot, up_hidhot = slot_tables(
        up_layout, count_trio[0], width_blocks
    )
    gate_major, gate_minor, gate_live, gate_rowhot, gate_hidhot = slot_tables(
        gate_layout, count_trio[1], width_blocks
    )
    down_major, down_minor, down_live, down_colhot, down_hidhot = slot_tables(
        down_layout, count_trio[2], width_blocks
    )
    w_up = up_blocks * up_live[:, None, None].astype(jnp.bfloat16)
    w_gate = gate_blocks * gate_live[:, None, None].astype(jnp.bfloat16)
    w_down = down_blocks * down_live[:, None, None].astype(jnp.bfloat16)
    x_up = jnp.take(x_split, up_major, axis=1)
    x_gate = jnp.take(x_split, gate_major, axis=1)
    up_terms = jnp.einsum("tsi,sij->tsj", x_up, w_up, preferred_element_type=f32)
    gate_terms = jnp.einsum("tsi,sij->tsj", x_gate, w_gate, preferred_element_type=f32)
    up_value = jnp.einsum("tsj,sh->thj", up_terms, up_hidhot, precision=highest)
    gate_value = jnp.einsum("tsj,sh->thj", gate_terms, gate_hidhot, precision=highest)
    sig = 1.0 / (1.0 + jnp.exp(-gate_value))
    act = gate_value * sig
    hidden = (act * up_value).astype(jnp.bfloat16)
    hid_down = jnp.take(hidden, down_minor, axis=1)
    out_terms = jnp.einsum("tsj,sjk->tsk", hid_down, w_down, preferred_element_type=f32)
    partial_out = jnp.einsum("tsk,sc->tck", out_terms, down_colhot, precision=highest).reshape(
        row_total, -1
    )
    out_share = lax.psum_scatter(partial_out, "tensor", scatter_dimension=0, tiled=True)
    dy_split = dy_full.reshape(row_total, width_blocks, block_size)
    dy_down = jnp.take(dy_split, down_major, axis=1)
    dh_terms = jnp.einsum("tsk,sjk->tsj", dy_down, w_down, preferred_element_type=f32)
    d_hidden = jnp.einsum("tsj,sh->thj", dh_terms, down_hidhot, precision=highest)
    d_up = (d_hidden * act).astype(jnp.bfloat16)
    d_gate = (d_hidden * up_value * sig * (1.0 + gate_value * (1.0 - sig))).astype(jnp.bfloat16)
    dup_slots = jnp.take(d_up, up_minor, axis=1)
    dgate_slots = jnp.take(d_gate, gate_minor, axis=1)
    dx_up = jnp.einsum("tsj,sij->tsi", dup_slots, w_up, preferred_element_type=f32)
    dx_gate = jnp.einsum("tsj,sij->tsi", dgate_slots, w_gate, preferred_element_type=f32)
    partial_dx = jnp.einsum("tsi,sr->tri", dx_up, up_rowhot, precision=highest)
    partial_dx = partial_dx + jnp.einsum("tsi,sr->tri", dx_gate, gate_rowhot, precision=highest)
    partial_dx = partial_dx.reshape(row_total, -1)
    dx_share = lax.psum_scatter(partial_dx, "tensor", scatter_dimension=0, tiled=True)
    grad_up = (
        jnp.einsum("tsi,tsj->sij", x_up, dup_slots, preferred_element_type=f32)
        * up_live[:, None, None]
    ).astype(jnp.bfloat16)
    grad_gate = (
        jnp.einsum("tsi,tsj->sij", x_gate, dgate_slots, preferred_element_type=f32)
        * gate_live[:, None, None]
    ).astype(jnp.bfloat16)
    grad_down = (
        jnp.einsum("tsj,tsk->sjk", hid_down, dy_down, preferred_element_type=f32)
        * down_live[:, None, None]
    ).astype(jnp.bfloat16)
    return (
        out_share.astype(jnp.bfloat16),
        dx_share.astype(jnp.bfloat16),
        grad_up,
        grad_gate,
        grad_down,
    )


def solution(mesh):
    placed = (
        P(("groups", "tensor"), None),
        P(("groups", "tensor"), None),
        P("tensor", None, None),
        P("tensor", None, None),
        P("tensor", None, None),
        P("tensor"),
        P("tensor"),
        P("tensor"),
        P(None, "tensor"),
    )
    return jax.shard_map(
        local,
        mesh=mesh,
        in_specs=placed,
        out_specs=(
            P(("groups", "tensor"), None),
            P(("groups", "tensor"), None),
            P(("groups", "tensor"), None, None),
            P(("groups", "tensor"), None, None),
            P(("groups", "tensor"), None, None),
        ),
        check_vma=False,
    )
```

profile of v0, /device:TPU:0, one launch (start us, length us, event | category | flops | bytes accessed | tf_op | source)
XLA Modules:
  0.0 150.8 jit_solution(14236068998945516922)
XLA Ops:
  0.6 0.7 compare_and_fusion.1
  1.3 24.8 %all-gather = bf16[16,2,8192]{2,1,0:T(2,128)(2,1)S(1)} all-gather(bf16[1,2,8192]{2,1,0:T(2,128)(2,1)} %bitcast.118), channel_id=1, replica_groups=mesh['groups'=2,'tensor'=16] {'tensor'}, dimensions={0}, use_global_device_ids=true | all-gather | bytes 557056 | tf_op jit(solution)/shard_map/all_gather | solution.py:32
  26.1 0.4 reshape.71
  26.5 0.0 copy-start.4
  26.5 0.0 copy-start
  26.5 0.3 copy.44
  26.9 0.6 gather_fusion.1
  27.5 0.0 copy-done.4
  27.5 0.6 fusion.74
  28.1 0.6 fusion.73
  28.8 0.0 copy-done
  28.8 0.0 copy-start.5
  28.8 0.5 convolution_bitcast_fusion.1
  29.3 0.6 fusion.13
  29.8 0.0 copy-done.5
  29.9 0.6 gather_fusion
  30.5 0.6 fusion.72
  31.2 0.0 copy-start.6
  31.2 0.0 copy-start.3
  31.2 1.7 %convolution_bitcast_fusion.2 = f32[32,32,128]{2,0,1:T(8,128)S(1)} fusion(bf16[32,128,128]{2,1,0:T(8,128)(2,1)} %param.16, bf16[32]{0:T(256)(128)(2,1)S(1)} %fusion.72, bf16[32,32,128]{2,1,0:T(8,128)(2,1)S(1)} %gather_fusion, pred[32]{0:T(512)(128)(4,1)S(1)} %get-tuple-element.26), kind=kOutput, calls=%fused_computation.12 | convolution fusion | flops 35782656 | bytes 1835104 | tf_op jit(solution)/shard_map/tsi,sij->tsj/dot_general | solution.py:54
  32.9 0.6 fusion.15
  33.5 0.0 copy-done.6
  33.5 0.0 copy-done.3
  33.5 18.9 %all-gather.1 = bf16[16,2,8192]{2,1,0:T(2,128)(2,1)S(1)} all-gather(bf16[1,2,8192]{2,1,0:T(2,128)(2,1)S(1)} %bitcast.119), channel_id=1, replica_groups=mesh['groups'=2,'tensor'=16] {'tensor'}, dimensions={0}, use_global_device_ids=true | all-gather | bytes 557056 | tf_op jit(solution)/shard_map/all_gather | solution.py:33
  52.4 0.4 reshape.73
  52.8 0.3 copy.51
  53.2 0.6 gather_fusion.3
  53.8 0.6 fusion.71
  54.3 1.9 %convolution_bitcast_fusion.5 = f32[32,32,128]{2,0,1:T(8,128)S(1)} fusion(bf16[32,128,128]{2,1,0:T(8,128)(2,1)} %param.17, bf16[32]{0:T(256)(128)(2,1)S(1)} %fusion.71, bf16[32,32,128]{2,1,0:T(8,128)(2,1)S(1)} %gather_fusion.3, pred[32]{0:T(512)(128)(4,1)S(1)} %get-tuple-element.13), kind=kOutput, calls=%fused_computation.15 | convolution fusion | flops 34209792 | bytes 1835104 | tf_op jit(solution)/shard_map/tsk,sjk->tsj/dot_general | solution.py:68
  56.3 0.6 fusion.9
  57.0 0.6 gather_fusion.4
  57.6 0.7 convolution_bitcast_fusion.4
  58.3 0.0 copy-start.1
  58.3 0.9 fusion.7
  59.3 1.3 gather_fusion.5
  60.6 0.0 copy-done.1
  60.6 1.7 %convolution_bitcast_fusion.3 = f32[32,32,128]{2,0,1:T(8,128)S(1)} fusion(bf16[32,128,128]{2,1,0:T(8,128)(2,1)S(1)} %copy-done.1, bf16[32]{0:T(256)(128)(2,1)S(1)} %fusion.72, bf16[32,32,128]{2,1,0:T(8,128)(2,1)} %gather_fusion.5, pred[32]{0:T(512)(128)(4,1)S(1)} %get-tuple-element.9), kind=kOutput, calls=%fused_computation.13 | convolution fusion | flops 34209792 | bytes 1835104 | tf_op jit(solution)/shard_map/tsj,sij->tsi/dot_general | solution.py:75
  62.2 1.0 convolution_add_fusion
  63.2 0.0 copy-start.2
  63.2 0.6 copy.82
  63.9 0.6 gather_fusion.2
  64.5 0.0 copy-done.2
  64.5 0.5 convolution_bitcast_fusion
  65.0 0.9 fusion.11
  65.9 0.6 copy.83
  66.5 0.0 copy-start.7
  66.5 73.7 %all-reduce.4 = (bf16[32,8192]{1,0:T(8,128)(2,1)}, bf16[32,8192]{1,0:T(8,128)(2,1)}) all-reduce(f32[32,8192]{1,0:T(8,128)S(1)} %bitcast.115, f32[32,8192]{1,0:T(8,128)S(1)} %bitcast.114), channel_id=2, replica_groups=mesh['groups'=2,'tensor'=16] {'tensor'}, use_global_device_ids=true, to_apply=%region_0.3.clone | all-reduce | flops 524288 | bytes 3145728
  140.2 0.0 copy-done.7
  140.2 0.6 dynamic-slice
  141.4 1.7 %dynamic-slice_convert_fusion = (bf16[2,8192]{1,0:T(2,128)(2,1)}, bf16[2,8192]{1,0:T(2,128)(2,1)}) fusion(bf16[32,8192]{1,0:T(8,128)(2,1)} %get-tuple-element.8, u32[]{:T(128)S(6)} %multiply.1, bf16[32,8192]{1,0:T(8,128)(2,1)} %get-tuple-element.7), kind=kLoop, calls=%fused_computation.59 | loop fusion | bytes 131076 | tf_op jit(solution)/shard_map/convert_element_type | solution.py:94
  143.1 0.6 compare_convert_fusion.1
  143.8 2.6 %multiply_convert_fusion.1 = bf16[32,128,128]{2,1,0:T(8,128)(2,1)} fusion(f32[32]{0:T(128)S(1)} %compare_convert_fusion.1, bf16[32,32,128]{2,1,0:T(8,128)(2,1)S(1)} %gather_fusion, pred[32]{0:T(512)(128)(4,1)S(1)} %get-tuple-element.26, bf16[32,32,128]{2,1,0:T(8,128)(2,1)} %gather_fusion.5, pred[32]{0:T(512)(128)(4,1)S(1)} %get-tuple-element.9), kind=kOutput, calls=%fused_computation.7 | convolution fusion | flops 34865152 | bytes 1573056 | tf_op jit(solution)/shard_map/tsi,tsj->sij/dot_general | solution.py:85
  146.3 0.6 compare_convert_fusion
  147.0 1.6 %multiply_convert_fusion.2 = bf16[32,128,128]{2,1,0:T(8,128)(2,1)} fusion(f32[32]{0:T(128)S(1)} %compare_convert_fusion, bf16[32,32,128]{2,1,0:T(8,128)(2,1)S(1)} %gather_fusion.1, pred[32]{0:T(512)(128)(4,1)S(1)} %get-tuple-element.31, bf16[32,32,128]{2,1,0:T(8,128)(2,1)S(1)} %gather_fusion.4, pred[32]{0:T(512)(128)(4,1)S(1)} %get-tuple-element.11), kind=kOutput, calls=%fused_computation.8 | convolution fusion | flops 34865152 | bytes 1573056 | tf_op jit(solution)/shard_map/tsi,tsj->sij/dot_general | solution.py:81
  148.6 0.6 compare_convert_fusion.2
  149.2 1.6 %multiply_convert_fusion = bf16[32,128,128]{2,1,0:T(8,128)(2,1)} fusion(f32[32]{0:T(128)S(1)} %compare_convert_fusion.2, bf16[32,32,128]{2,1,0:T(8,128)(2,1)S(1)} %gather_fusion.2, pred[32]{0:T(512)(128)(4,1)S(1)} %get-tuple-element.24, bf16[32,32,128]{2,1,0:T(8,128)(2,1)S(1)} %gather_fusion.3, pred[32]{0:T(512)(128)(4,1)S(1)} %get-tuple-element.13), kind=kOutput, calls=%fused_computation.6 | convolution fusion | flops 34865152 | bytes 1573056 | tf_op jit(solution)/shard_map/tsj,tsk->sjk/dot_general | solution.py:89
  (15 shorter events, 0.1 us)
Async XLA Ops:
  26.5 1.0 copy-start.4
  26.5 2.2 %copy-start = (bf16[32,128,128]{2,1,0:T(8,128)(2,1)S(1)}, bf16[32,128,128]{2,1,0:T(8,128)(2,1)}, u32[]{:S(2)}) copy-start(bf16[32,128,128]{2,1,0:T(8,128)(2,1)} %param.15) | copy-start | bytes 3145732
  28.8 1.1 copy-start.5
  31.2 2.3 %copy-start.6 = (s32[32]{0:T(128)S(1)}, s32[32]{0:T(128)}, u32[]{:S(2)}) copy-start(s32[32]{0:T(128)} %param.20) | copy-start | bytes 388
  31.2 2.4 %copy-start.3 = (bf16[2,8192]{1,0:T(2,128)(2,1)S(1)}, bf16[2,8192]{1,0:T(2,128)(2,1)}, u32[]{:S(2)}) copy-start(bf16[2,8192]{1,0:T(2,128)(2,1)} %param.14) | copy-start | bytes 98308
  58.3 2.3 %copy-start.1 = (bf16[32,128,128]{2,1,0:T(8,128)(2,1)S(1)}, bf16[32,128,128]{2,1,0:T(8,128)(2,1)}, u32[]{:S(2)}) copy-start(bf16[32,128,128]{2,1,0:T(8,128)(2,1)} %param.16) | copy-start | bytes 3145732
  63.2 1.3 copy-start.2
  66.5 73.7 %copy-start.7 = (u32[32]{0:T(128)S(1)}, u32[32]{0:T(128)}, u32[]{:S(2)}) copy-start(u32[32]{0:T(128)} %constant.59) | copy-start | bytes 388
where the time goes:
time: 151 us
  blocking collectives  117 us (77%)
  matrix products  17.4 us (12%)
  local copies, waits for them, and re-layouts  9.91 us (7%)
  other arithmetic  4.48 us (3%)
  between operations  1.65 us (1%)
    unnamed x1, blocking collectives  73.7 us
    all_gather x1, blocking collectives, local(): x_full = lax.all_gather(tokens, 'tensor', axis=0, tiled=True)  24.8 us
    all_gather x1, blocking collectives, local(): dy_full = lax.all_gather(cotangent, 'tensor', axis=0, tiled=True)  18.9 us

commit v1 on v0

--- a/solution.py
+++ b/solution.py
@@ -2,6 +2,7 @@
 import jax.numpy as jnp
 from jax import lax
 from jax.sharding import PartitionSpec as P
+from jax.lax import all_gather
 
 HB_DEV = 3
 
@@ -29,8 +30,11 @@
 ):
     highest = lax.Precision.HIGHEST
     f32 = jnp.float32
-    x_full = lax.all_gather(tokens, "tensor", axis=0, tiled=True)
-    dy_full = lax.all_gather(cotangent, "tensor", axis=0, tiled=True)
+    x_full, dy_full = jnp.split(
+        all_gather(jnp.concatenate([tokens, cotangent], axis=1), "tensor", axis=0, tiled=True),
+        [tokens.shape[1]],
+        axis=1,
+    )
     row_total = x_full.shape[0]
     block_size = up_blocks.shape[1]
     width_blocks = x_full.shape[1] // block_size

time: 151 us -> 161 us (1.066)
  blocking collectives: 117 us -> 73.7 us
  waiting for transfers between devices: 0 us -> 33.4 us
  between operations: 1.65 us -> 15 us
  local copies, waits for them, and re-layouts: 9.91 us -> 13.4 us
  other arithmetic: 4.48 us -> 7.49 us
    all_gather x2 -> x0, blocking collectives: 43.7 us -> none  [the longest x1 24.8 us: local(): x_full = lax.all_gather(tokens, 'tensor', axis=0, tiled=True)]
    all_gather x0 -> x1, waiting for transfers between devices: none -> 33.3 us  [local(): all_gather(jnp.concatenate([tokens, cotangent], axis=1), 'tensor', axis=0...]
    unnamed x19 -> x11, local copies, waits for them, and re-layouts: 1.85 us -> 4.43 us
  transfers between devices with their start and end apart: 0 -> 1, of which waited for: 0 -> 1; matrix products, arithmetic and copies ran while one was open for 0% -> 5% of each run, Pallas kernels for 0% -> 0%
where the time goes in v1:
time: 161 us; the launch traced here: 160 us
  blocking collectives  73.7 us (46%)
  waiting for transfers between devices  33.4 us (21%)
  matrix products  17.4 us (11%)
  between operations  15 us (9%)
  local copies, waits for them, and re-layouts  13.4 us (8%)
  other arithmetic  7.49 us (5%)
    unnamed x1, blocking collectives  73.7 us
    all_gather x1, waiting for transfers between devices, local(): all_gather(jnp.concatenate([tokens, cotangent], axis=1), 'tensor', axis=0...  33.3 us
    unnamed x11, local copies, waits for them, and re-layouts  4.43 us
  transfers between devices with their start and end apart: 1, of which 1 were waited for; matrix products, arithmetic and copies ran while one was open for 5% of the time, Pallas kernels for 0%

profile of v1, /device:TPU:0, one launch (start us, length us, event | category | flops | bytes accessed | tf_op | source)
XLA Modules:
  0.0 160.3 jit_solution(4732375541338344880)
XLA Ops:
  7.2 0.0 all-gather.3.cloned.1.call-start
  7.2 1.5 maximum_bitcast_fusion
  8.7 0.0 all-gather.3.cloned.1.call-update
  8.7 1.4 fusion.74
  10.1 0.6 fusion.72
  10.7 0.7 compare_convert_fusion.1
  11.4 0.7 fusion.73
  12.0 0.7 compare_convert_fusion
  12.7 0.7 fusion.71
  13.4 0.7 compare_convert_fusion.2
  14.0 1.2 dynamic-slice
  15.9 0.7 compare_and_fusion.1
  16.6 0.7 compare_and_fusion
  17.3 0.7 compare_and_fusion.2
  18.1 33.3 %all-gather.3.cloned.1.call-done = bf16[16,2,16384]{2,1,0:T(2,128)(2,1)} async-done(((bf16[1,2,16384]{2,1,0:T(2,128)(2,1)}), bf16[16,2,16384]{2,1,0:T(2,128)(2,1)}) %all-gather.3.cloned.1.call-update) | async-done | bytes 1048592 | tf_op jit(solution)/shard_map/all_gather | solution.py:34
  51.4 1.5 reshape.130
  52.9 0.1 slice_bitcast_fusion
  53.0 0.0 copy-start
  53.0 0.2 copy_bitcast_fusion.2
  53.2 0.6 gather_fusion.1
  53.8 0.4 copy-done
  54.2 0.5 convolution_bitcast_fusion.1
  54.6 0.6 fusion.13
  55.2 0.6 gather_fusion
  55.8 1.7 %convolution_bitcast_fusion.2 = f32[32,32,128]{2,0,1:T(8,128)S(1)} fusion(bf16[32,128,128]{2,1,0:T(8,128)(2,1)} %param.16, bf16[32]{0:T(256)(128)(2,1)S(1)} %fusion.72, bf16[32,32,128]{2,1,0:T(8,128)(2,1)S(1)} %gather_fusion, pred[32]{0:T(512)(128)(4,1)S(1)} %get-tuple-element.28), kind=kOutput, calls=%fused_computation.12 | convolution fusion | flops 35782656 | bytes 1835104 | tf_op jit(solution)/shard_map/tsi,sij->tsj/dot_general | solution.py:58
  57.5 0.6 fusion.15
  58.1 0.6 gather_fusion.3
  58.7 1.9 %convolution_bitcast_fusion.5 = f32[32,32,128]{2,0,1:T(8,128)S(1)} fusion(bf16[32,128,128]{2,1,0:T(8,128)(2,1)} %param.17, bf16[32]{0:T(256)(128)(2,1)S(1)} %fusion.71, bf16[32,32,128]{2,1,0:T(8,128)(2,1)S(1)} %gather_fusion.3, pred[32]{0:T(512)(128)(4,1)S(1)} %get-tuple-element.13), kind=kOutput, calls=%fused_computation.15 | convolution fusion | flops 34209792 | bytes 1835104 | tf_op jit(solution)/shard_map/tsk,sjk->tsj/dot_general | solution.py:72
  60.7 0.6 fusion.9
  61.3 0.6 gather_fusion.4
  61.9 0.7 convolution_bitcast_fusion.4
  62.6 0.0 copy-start.1
  62.6 0.9 fusion.7
  63.6 1.3 gather_fusion.5
  64.9 0.0 copy-done.1
  64.9 1.7 %convolution_bitcast_fusion.3 = f32[32,32,128]{2,0,1:T(8,128)S(1)} fusion(bf16[32,128,128]{2,1,0:T(8,128)(2,1)S(1)} %copy-done.1, bf16[32]{0:T(256)(128)(2,1)S(1)} %fusion.72, bf16[32,32,128]{2,1,0:T(8,128)(2,1)} %gather_fusion.5, pred[32]{0:T(512)(128)(4,1)S(1)} %get-tuple-element.9), kind=kOutput, calls=%fused_computation.13 | convolution fusion | flops 34209792 | bytes 1835104 | tf_op jit(solution)/shard_map/tsj,sij->tsi/dot_general | solution.py:79
  66.6 0.9 convolution_add_fusion
  67.5 0.0 copy-start.2
  67.5 0.6 copy.86
  68.1 0.6 gather_fusion.2
  68.8 0.0 copy-done.2
  68.8 0.5 convolution_bitcast_fusion
  69.2 0.9 fusion.11
  70.2 0.6 copy.87
  70.8 73.7 %all-reduce.4 = (bf16[32,8192]{1,0:T(8,128)(2,1)}, bf16[32,8192]{1,0:T(8,128)(2,1)}) all-reduce(f32[32,8192]{1,0:T(8,128)S(1)} %bitcast.123, f32[32,8192]{1,0:T(8,128)S(1)} %bitcast.122), channel_id=2, replica_groups=mesh['groups'=2,'tensor'=16] {'tensor'}, use_global_device_ids=true, to_apply=%region_0.3.clone | all-reduce | flops 524288 | bytes 3145728
  144.5 1.6 dynamic-slice_convert_fusion
  146.1 1.6 dynamic-slice_convert_fusion.1
  147.6 2.6 %multiply_convert_fusion.1 = bf16[32,128,128]{2,1,0:T(8,128)(2,1)} fusion(f32[32]{0:T(128)S(1)} %compare_convert_fusion.1, bf16[32,32,128]{2,1,0:T(8,128)(2,1)S(1)} %gather_fusion, pred[32]{0:T(512)(128)(4,1)S(1)} %get-tuple-element.28, bf16[32,32,128]{2,1,0:T(8,128)(2,1)} %gather_fusion.5, pred[32]{0:T(512)(128)(4,1)S(1)} %get-tuple-element.9), kind=kOutput, calls=%fused_computation.7 | convolution fusion | flops 34865152 | bytes 1573056 | tf_op jit(solution)/shard_map/tsi,tsj->sij/dot_general | solution.py:89
  150.2 1.6 %multiply_convert_fusion.2 = bf16[32,128,128]{2,1,0:T(8,128)(2,1)} fusion(f32[32]{0:T(128)S(1)} %compare_convert_fusion, bf16[32,32,128]{2,1,0:T(8,128)(2,1)S(1)} %gather_fusion.1, pred[32]{0:T(512)(128)(4,1)S(1)} %get-tuple-element.33, bf16[32,32,128]{2,1,0:T(8,128)(2,1)S(1)} %gather_fusion.4, pred[32]{0:T(512)(128)(4,1)S(1)} %get-tuple-element.11), kind=kOutput, calls=%fused_computation.8 | convolution fusion | flops 34865152 | bytes 1573056 | tf_op jit(solution)/shard_map/tsi,tsj->sij/dot_general | solution.py:85
  151.9 1.6 %multiply_convert_fusion = bf16[32,128,128]{2,1,0:T(8,128)(2,1)} fusion(f32[32]{0:T(128)S(1)} %compare_convert_fusion.2, bf16[32,32,128]{2,1,0:T(8,128)(2,1)S(1)} %gather_fusion.2, pred[32]{0:T(512)(128)(4,1)S(1)} %get-tuple-element.26, bf16[32,32,128]{2,1,0:T(8,128)(2,1)S(1)} %gather_fusion.3, pred[32]{0:T(512)(128)(4,1)S(1)} %get-tuple-element.13), kind=kOutput, calls=%fused_computation.6 | convolution fusion | flops 34865152 | bytes 1573056 | tf_op jit(solution)/shard_map/tsj,tsk->sjk/dot_general | solution.py:93
  (10 shorter events, 0.1 us)
Async XLA Ops:
  7.2 44.2 %all-gather.3.cloned.1.call-start = ((), (), s32[]{:S(2)}) async-start(), calls=%async_computation | async-start | bytes 1114112 | tf_op jit(solution)/shard_map/all_gather | solution.py:34
  53.0 1.2 copy-start
  62.6 2.2 %copy-start.1 = (bf16[32,128,128]{2,1,0:T(8,128)(2,1)S(1)}, bf16[32,128,128]{2,1,0:T(8,128)(2,1)}, u32[]{:S(2)}) copy-start(bf16[32,128,128]{2,1,0:T(8,128)(2,1)} %param.16) | copy-start | bytes 3145732
  67.5 1.2 copy-start.2
Sparse Core Ops, SparseCore 0:
  10.7 40.6 all-gather.2
